TPU v7x, 32 devices: a whole 2x2x4 slice. The times are simulated.
32 devices in a mesh: dp: 8 (over y, x, core), tensor: 4 (over z).
Axes of the slice: x: 2, y: 2, z: 4, core: 2. Of those that a mesh axis runs over, the one named last changes fastest.
Arguments:
- block_input: float32 [8, 736, 1152], P('dp', 'tensor'), may hold values from -6 to 6
- key_valid: int32 [8, 736], P('dp'), may hold values from 0 to 1, as said below
- mixgain: bfloat16 [2, 1152], P(None, 'dp'), may hold values from 0.5 to 1.5
- mixbias: bfloat16 [2, 1152], P(None, 'dp'), may hold values from -3 to 3
- inproj_weight: bfloat16 [2, 3, 1152, 1152], P(None, None, 'dp', 'tensor'), may hold values from -1 to 1
- querybias: bfloat16 [2, 1152], P(None, 'tensor'), may hold values from -3 to 3
- valuebias: bfloat16 [2, 1152], P(None, 'tensor'), may hold values from -3 to 3
- outproj_weight: bfloat16 [2, 1152, 1152], P(None, 'tensor', 'dp'), may hold values from -3 to 3
- outbias: bfloat16 [2, 1152], P(None, 'dp'), may hold values from -3 to 3
- ffgain: bfloat16 [2, 1152], P(None, 'dp'), may hold values from 0.5 to 1.5
- ffbias: bfloat16 [2, 1152], P(None, 'dp'), may hold values from -3 to 3
- expand_weight: bfloat16 [2, 1152, 4304], P(None, 'dp', 'tensor'), may hold values from -0.1875 to 0.1875
- expbias: bfloat16 [2, 4304], P(None, 'tensor'), may hold values from -3 to 3
- contract_weight: bfloat16 [2, 4304, 1152], P(None, 'tensor', 'dp'), may hold values from -0.25 to 0.25
- conbias: bfloat16 [2, 1152], P(None, 'dp'), may hold values from -4 to 4
- cotangent: float32 [8, 736, 1152], P('dp', 'tensor'), may hold values from -6 to 6
Outputs:
- block_output: float32 [8, 736, 1152], P('dp', 'tensor')
- input_gradient: float32 [8, 736, 1152], P('dp', 'tensor')
- mixgain_gradient: float32 [2, 1152], P(None, 'dp')
- mixbias_gradient: float32 [2, 1152], P(None, 'dp')
- inproj_gradient: float32 [2, 3, 1152, 1152], P(None, None, 'dp', 'tensor')
- querybias_gradient: float32 [2, 1152], P(None, 'tensor')
- valuebias_gradient: float32 [2, 1152], P(None, 'tensor')
- outproj_gradient: float32 [2, 1152, 1152], P(None, 'tensor', 'dp')
- outbias_gradient: float32 [2, 1152], P(None, 'dp')
- ffgain_gradient: float32 [2, 1152], P(None, 'dp')
- ffbias_gradient: float32 [2, 1152], P(None, 'dp')
- expand_gradient: float32 [2, 1152, 4304], P(None, 'dp', 'tensor')
- expbias_gradient: float32 [2, 4304], P(None, 'tensor')
- contract_gradient: float32 [2, 4304, 1152], P(None, 'tensor', 'dp')
- conbias_gradient: float32 [2, 1152], P(None, 'dp')
Inputs may be any that keep to these rules, and one draw needn't show every extreme that they name: `key_valid`: each image's row is 1 on a first run of positions and 0 after it; every image has from 552 to 736 ones, and both ends occur in every draw.
All inputs are finite; a program needn't handle non-finite values.
Results may differ from a plain program's by a relative error of at most 0.033.
Values may be sent and summed in bfloat16 or wider, within the bound.
A program may use at most 192 MiB of HBM per device.

v0:
```python
import jax
import jax.numpy as jnp
from jax import lax
from jax.sharding import PartitionSpec as P

HEAD_DIM = 72


norm_epsilon = 1e-06
gelu_scale = 0.7978845608028654
gelu_cubic = 0.044715
masked_score = -1e30


def layer_norm(matrix_rows, norm_gain, norm_shift):
    centered = matrix_rows - jnp.mean(matrix_rows, axis=-1, keepdims=True)
    inverse = lax.rsqrt(jnp.mean(centered * centered, axis=-1, keepdims=True) + norm_epsilon)
    normed = centered * inverse
    return (
        normed * norm_gain.astype(jnp.float32) + norm_shift.astype(jnp.float32),
        normed,
        inverse,
    )


def norm_backward(upstream, normed, inverse, norm_gain):
    scaled = upstream * norm_gain.astype(jnp.float32)
    mean_first = jnp.mean(scaled, axis=-1, keepdims=True)
    mean_second = jnp.mean(scaled * normed, axis=-1, keepdims=True)
    return inverse * (scaled - mean_first - normed * mean_second)


def gelu_parts(preact):
    tanh_part = jnp.tanh(gelu_scale * (preact + gelu_cubic * preact * preact * preact))
    gelu_value = 0.5 * preact * (1.0 + tanh_part)
    gelu_slope = 0.5 * (1.0 + tanh_part) + 0.5 * preact * (
        1.0 - tanh_part * tanh_part
    ) * gelu_scale * (1.0 + 3.0 * gelu_cubic * preact * preact)
    return (gelu_value, gelu_slope)


def masked_scores(queries, keys_half, usable, factor):
    scores = (
        jnp.einsum("bqhd,bkhd->bhqk", queries, keys_half, preferred_element_type=jnp.float32)
        * factor
    )
    return jnp.where(usable[:, None, None, :], scores, masked_score)


def attend(queries, keys_half, values_half, usable, factor):
    scores = masked_scores(queries, keys_half, usable, factor)
    highest = jnp.max(scores, axis=-1, keepdims=True)
    log_total = highest + jnp.log(jnp.sum(jnp.exp(scores - highest), axis=-1, keepdims=True))
    weights = jnp.exp(scores - log_total).astype(jnp.bfloat16)
    mixed_out = jnp.einsum(
        "bhqk,bkhd->bqhd", weights, values_half, preferred_element_type=jnp.float32
    )
    return (mixed_out.astype(jnp.bfloat16), log_total)


def attend_backward(queries, keys_half, values_half, usable, log_total, upstream, factor):
    weights = jnp.exp(masked_scores(queries, keys_half, usable, factor) - log_total)
    value_grad = jnp.einsum(
        "bhqk,bqhd->bkhd",
        weights.astype(jnp.bfloat16),
        upstream,
        preferred_element_type=jnp.float32,
    )
    weight_grad = jnp.einsum(
        "bqhd,bkhd->bhqk", upstream, values_half, preferred_element_type=jnp.float32
    )
    inner_sum = jnp.sum(weights * weight_grad, axis=-1, keepdims=True)
    score_grad = (weights * (weight_grad - inner_sum) * factor).astype(jnp.bfloat16)
    query_grad = jnp.einsum(
        "bhqk,bkhd->bqhd", score_grad, keys_half, preferred_element_type=jnp.float32
    )
    key_grad = jnp.einsum(
        "bhqk,bqhd->bkhd", score_grad, queries, preferred_element_type=jnp.float32
    )
    return (query_grad, key_grad, value_grad)


def body(
    block_input,
    key_valid,
    mixgain,
    mixbias,
    inproj_weight,
    querybias,
    valuebias,
    outproj_weight,
    outbias,
    ffgain,
    ffbias,
    expand_weight,
    expbias,
    contract_weight,
    conbias,
    cotangent,
):
    images = block_input.shape[0]
    model_width = block_input.shape[2]
    seq_total = key_valid.shape[1]
    depth_count = inproj_weight.shape[0]
    local_width = inproj_weight.shape[-1]
    local_heads = local_width // HEAD_DIM
    local_hidden = expand_weight.shape[-1]
    hidden_total = local_hidden * lax.axis_size("tensor")
    shard_width = model_width // lax.axis_size("dp")
    factor = float(HEAD_DIM) ** (-0.5)
    usable = key_valid > 0
    tensor_index = lax.axis_index("tensor")
    data_index = lax.axis_index("dp")
    head_shape = (images, seq_total, local_heads, HEAD_DIM)

    def fetch_attention(layer_index):
        return (
            lax.all_gather(inproj_weight[layer_index], "dp", axis=1, tiled=True),
            lax.all_gather(outproj_weight[layer_index], "dp", axis=1, tiled=True),
            lax.all_gather(mixgain[layer_index], "dp", axis=0, tiled=True),
            lax.all_gather(mixbias[layer_index], "dp", axis=0, tiled=True),
            lax.all_gather(outbias[layer_index], "dp", axis=0, tiled=True),
        )

    def fetch_dense(layer_index):
        return (
            lax.all_gather(expand_weight[layer_index], "dp", axis=0, tiled=True),
            lax.all_gather(contract_weight[layer_index], "dp", axis=1, tiled=True),
            lax.all_gather(ffgain[layer_index], "dp", axis=0, tiled=True),
            lax.all_gather(ffbias[layer_index], "dp", axis=0, tiled=True),
            lax.all_gather(conbias[layer_index], "dp", axis=0, tiled=True),
        )

    residual = block_input
    stored = []
    for layer_index in range(depth_count):
        attention_pack = fetch_attention(layer_index)
        inproj_full, outproj_full, mix_gain, mix_shift, out_shift = attention_pack
        mix_value, mix_normed, mix_inverse = layer_norm(residual, mix_gain, mix_shift)
        mix_rows = lax.all_gather(mix_value.astype(jnp.bfloat16), "tensor", axis=1, tiled=True)
        projected = jnp.einsum(
            "bsd,cde->cbse", mix_rows, inproj_full, preferred_element_type=jnp.float32
        )
        queries = (
            (projected[0] + querybias[layer_index].astype(jnp.float32))
            .astype(jnp.bfloat16)
            .reshape(head_shape)
        )
        keys_half = projected[1].astype(jnp.bfloat16).reshape(head_shape)
        values_half = (
            (projected[2] + valuebias[layer_index].astype(jnp.float32))
            .astype(jnp.bfloat16)
            .reshape(head_shape)
        )
        heads_out, log_total = attend(queries, keys_half, values_half, usable, factor)
        heads_flat = heads_out.reshape(images, seq_total, local_width)
        partial_out = jnp.einsum(
            "bse,ed->bsd", heads_flat, outproj_full, preferred_element_type=jnp.float32
        )
        middle = (
            residual
            + lax.psum_scatter(
                partial_out.astype(jnp.bfloat16), "tensor", scatter_dimension=1, tiled=True
            ).astype(jnp.float32)
            + out_shift.astype(jnp.float32)
        )
        dense_pack = fetch_dense(layer_index)
        expand_full, contract_full, ff_gain, ff_shift, con_shift = dense_pack
        ff_value, ff_normed, ff_inverse = layer_norm(middle, ff_gain, ff_shift)
        ff_rows = lax.all_gather(ff_value.astype(jnp.bfloat16), "tensor", axis=1, tiled=True)
        preact = jnp.einsum(
            "bsd,df->bsf", ff_rows, expand_full, preferred_element_type=jnp.float32
        ) + expbias[layer_index].astype(jnp.float32)
        gelu_value, gelu_slope = gelu_parts(preact)
        hidden_half = gelu_value.astype(jnp.bfloat16)
        partial_dense = jnp.einsum(
            "bsf,fd->bsd", hidden_half, contract_full, preferred_element_type=jnp.float32
        )
        stored.append(
            (
                mix_normed,
                mix_inverse,
                mix_rows,
                queries,
                keys_half,
                values_half,
                log_total,
                heads_flat,
                ff_normed,
                ff_inverse,
                ff_rows,
                gelu_slope,
                hidden_half,
                attention_pack,
                dense_pack,
            )
        )
        residual = (
            middle
            + lax.psum_scatter(
                partial_dense.astype(jnp.bfloat16), "tensor", scatter_dimension=1, tiled=True
            ).astype(jnp.float32)
            + con_shift.astype(jnp.float32)
        )
    upstream = cotangent
    layer_results = [None] * depth_count
    for layer_index in reversed(range(depth_count)):
        (
            mix_normed,
            mix_inverse,
            mix_rows,
            queries,
            keys_half,
            values_half,
            log_total,
            heads_flat,
            ff_normed,
            ff_inverse,
            ff_rows,
            gelu_slope,
            hidden_half,
            attention_pack,
            dense_pack,
        ) = stored[layer_index]
        expand_full, contract_full, ff_gain, ff_shift, con_shift = fetch_dense(layer_index)
        upstream_half = upstream.astype(jnp.bfloat16)
        upstream_rows = lax.all_gather(upstream_half, "tensor", axis=1, tiled=True)
        contract_grad = jnp.einsum(
            "bsf,bsd->fd", hidden_half, upstream_rows, preferred_element_type=jnp.float32
        )
        preact_grad = (
            jnp.einsum(
                "bsd,fd->bsf", upstream_rows, contract_full, preferred_element_type=jnp.float32
            )
            * gelu_slope
        )
        preact_half = preact_grad.astype(jnp.bfloat16)
        expand_grad = jnp.einsum(
            "bsd,bsf->df", ff_rows, preact_half, preferred_element_type=jnp.float32
        )
        ff_partial = jnp.einsum(
            "bsf,df->bsd", preact_half, expand_full, preferred_element_type=jnp.float32
        )
        ff_back = lax.psum_scatter(
            ff_partial.astype(jnp.bfloat16), "tensor", scatter_dimension=1, tiled=True
        ).astype(jnp.float32)
        middle_grad = upstream + norm_backward(ff_back, ff_normed, ff_inverse, ff_gain)
        inproj_full, outproj_full, mix_gain, mix_shift, out_shift = fetch_attention(layer_index)
        middle_rows = lax.all_gather(middle_grad.astype(jnp.bfloat16), "tensor", axis=1, tiled=True)
        outproj_grad = jnp.einsum(
            "bse,bsd->ed", heads_flat, middle_rows, preferred_element_type=jnp.float32
        )
        heads_grad = (
            jnp.einsum("bsd,ed->bse", middle_rows, outproj_full, preferred_element_type=jnp.float32)
            .astype(jnp.bfloat16)
            .reshape(head_shape)
        )
        query_grad, key_grad, value_grad = attend_backward(
            queries, keys_half, values_half, usable, log_total, heads_grad, factor
        )
        proj_grad = jnp.stack([query_grad, key_grad, value_grad]).reshape(
            3, images, seq_total, local_width
        )
        proj_half = proj_grad.astype(jnp.bfloat16)
        inproj_grad = jnp.einsum(
            "bsd,cbse->cde", mix_rows, proj_half, preferred_element_type=jnp.float32
        )
        mix_partial = jnp.einsum(
            "cbse,cde->bsd", proj_half, inproj_full, preferred_element_type=jnp.float32
        )
        mix_back = lax.psum_scatter(
            mix_partial.astype(jnp.bfloat16), "tensor", scatter_dimension=1, tiled=True
        ).astype(jnp.float32)
        upstream_next = middle_grad + norm_backward(mix_back, mix_normed, mix_inverse, mix_gain)
        query_full = lax.dynamic_update_slice(
            jnp.zeros((model_width,), jnp.float32),
            jnp.sum(proj_grad[0], axis=(0, 1)),
            (tensor_index * local_width,),
        )
        value_full = lax.dynamic_update_slice(
            jnp.zeros((model_width,), jnp.float32),
            jnp.sum(proj_grad[2], axis=(0, 1)),
            (tensor_index * local_width,),
        )
        expand_full_bias = lax.dynamic_update_slice(
            jnp.zeros((hidden_total,), jnp.float32),
            jnp.sum(preact_grad, axis=(0, 1)),
            (tensor_index * local_hidden,),
        )
        vector_rows = jnp.stack(
            [
                jnp.sum(mix_back * mix_normed, axis=(0, 1)),
                jnp.sum(mix_back, axis=(0, 1)),
                jnp.sum(middle_grad, axis=(0, 1)),
                jnp.sum(ff_back * ff_normed, axis=(0, 1)),
                jnp.sum(ff_back, axis=(0, 1)),
                jnp.sum(upstream, axis=(0, 1)),
                query_full,
                value_full,
            ]
        )
        local_grads = (inproj_grad, outproj_grad, expand_grad, contract_grad)
        weight_parts = (
            lax.psum_scatter(
                local_grads[0].astype(jnp.bfloat16), "dp", scatter_dimension=1, tiled=True
            ).astype(jnp.float32),
            lax.psum_scatter(
                local_grads[1].astype(jnp.bfloat16), "dp", scatter_dimension=1, tiled=True
            ).astype(jnp.float32),
            lax.psum_scatter(
                local_grads[2].astype(jnp.bfloat16), "dp", scatter_dimension=0, tiled=True
            ).astype(jnp.float32),
            lax.psum_scatter(
                local_grads[3].astype(jnp.bfloat16), "dp", scatter_dimension=1, tiled=True
            ).astype(jnp.float32),
        )
        layer_results[layer_index] = (weight_parts, vector_rows, expand_full_bias)
        upstream = upstream_next
    inproj_list = []
    outproj_list = []
    expand_list = []
    contract_list = []
    vector_list = []
    expbias_list = []
    for position in range(depth_count):
        weight_parts, vector_rows, expand_full_bias = layer_results[position]
        inproj_list.append(weight_parts[0])
        outproj_list.append(weight_parts[1])
        expand_list.append(weight_parts[2])
        contract_list.append(weight_parts[3])
        vector_list.append(vector_rows)
        expbias_list.append(expand_full_bias)
    inproj_out, outproj_out, expand_out, contract_out = (
        jnp.stack(inproj_list),
        jnp.stack(outproj_list),
        jnp.stack(expand_list),
        jnp.stack(contract_list),
    )
    vector_total, expbias_total = lax.psum(
        (jnp.stack(vector_list), jnp.stack(expbias_list)), ("dp", "tensor")
    )
    data_part = lax.dynamic_slice_in_dim(vector_total, data_index * shard_width, shard_width, 2)
    tensor_part = lax.dynamic_slice_in_dim(vector_total, tensor_index * local_width, local_width, 2)
    expbias_part = lax.dynamic_slice_in_dim(
        expbias_total, tensor_index * local_hidden, local_hidden, 1
    )
    return (
        residual,
        upstream,
        data_part[:, 0],
        data_part[:, 1],
        inproj_out,
        tensor_part[:, 6],
        tensor_part[:, 7],
        outproj_out,
        data_part[:, 2],
        data_part[:, 3],
        data_part[:, 4],
        expand_out,
        expbias_part,
        contract_out,
        data_part[:, 5],
    )


def solution(mesh):
    return jax.shard_map(
        body,
        mesh=mesh,
        in_specs=(
            P("dp", "tensor", None),
            P("dp", None),
            P(None, "dp"),
            P(None, "dp"),
            P(None, None, "dp", "tensor"),
            P(None, "tensor"),
            P(None, "tensor"),
            P(None, "tensor", "dp"),
            P(None, "dp"),
            P(None, "dp"),
            P(None, "dp"),
            P(None, "dp", "tensor"),
            P(None, "tensor"),
            P(None, "tensor", "dp"),
            P(None, "dp"),
            P("dp", "tensor", None),
        ),
        out_specs=(
            P("dp", "tensor", None),
            P("dp", "tensor", None),
            P(None, "dp"),
            P(None, "dp"),
            P(None, None, "dp", "tensor"),
            P(None, "tensor"),
            P(None, "tensor"),
            P(None, "tensor", "dp"),
            P(None, "dp"),
            P(None, "dp"),
            P(None, "dp"),
            P(None, "dp", "tensor"),
            P(None, "tensor"),
            P(None, "tensor", "dp"),
            P(None, "dp"),
        ),
        check_vma=False,
    )
```

profile of v0, /device:TPU:8, one launch (start us, length us, event | category | flops | bytes accessed | tf_op | source)
XLA Modules:
  0.0 1476.0 jit_solution(15815517332685027929)
XLA Ops:
  19.3 24.6 %all-reduce.20 = (bf16[1152]{0:T(1024)(128)(2,1)S(1)}, bf16[1152]{0:T(1024)(128)(2,1)S(1)}, bf16[1152]{0:T(1024)(128)(2,1)S(1)}, bf16[1152]{0:T(1024)(128)(2,1)S...) all-reduce(bf16[1152]{0:T(1024)(128)(2,1)S(1)} %dynamic-update-slic, ...), channel_id=3, replica_groups=mesh['dp'=8,'tensor'=4] {'dp'}, use_global_device_ids=true, to_apply=%add.1 | all-reduce | flops 13824 | bytes 55296
  57.9 26.3 %all-gather.35.cloned.1.call-done = bf16[1,736,1152]{2,1,0:T(8,128)(2,1)} async-done(((bf16[1,184,1152]{2,1,0:T(8,128)(2,1)}), bf16[1,736,1152]{2,1,0:T(8,128)(2,1)}) %all-gather.35.cloned.1.call-update) | async-done | bytes 1695760 | tf_op jit(solution)/shard_map/all_gather | solution.py:140
  84.2 32.5 %all-gather.51.cloned.1.call-done = bf16[1,3,1152,288]{3,2,1,0:T(8,128)(2,1)} async-done(((bf16[1,3,144,288]{3,2,1,0:T(8,128)(2,1)}), bf16[1,3,1152,288]{3,2,1,0:T(8,128)(2,1)}) %all-gather.51.cloned.1.call-update) | async-done | bytes 1990672 | tf_op jit(solution)/shard_map/all_gather | solution.py:118
  135.5 35.4 %reduce-scatter.61.cloned.1.call-done = bf16[1,184,1152]{2,1,0:T(8,128)(2,1)} async-done(((bf16[1,736,1152]{2,1,0:T(8,128)(2,1)}), bf16[1,184,1152]{2,1,0:T(8,128)(2,1)}) %reduce-scatter.61.cloned.1.call-update) | async-done | bytes 423952
  174.8 28.7 %all-gather.53.cloned.1.call-done = bf16[1,1152,1076]{2,1,0:T(8,128)(2,1)} async-done(((bf16[1,144,1076]{2,1,0:T(8,128)(2,1)}), bf16[1,1152,1076]{2,1,0:T(8,128)(2,1)}) %all-gather.53.cloned.1.call-update) | async-done | bytes 2479120 | tf_op jit(solution)/shard_map/all_gather | solution.py:127
  203.5 40.1 %all-gather.37.cloned.1.call-done = bf16[1,736,1152]{2,1,0:T(8,128)(2,1)} async-done(((bf16[1,184,1152]{2,1,0:T(8,128)(2,1)}), bf16[1,736,1152]{2,1,0:T(8,128)(2,1)}) %all-gather.37.cloned.1.call-update) | async-done | bytes 1695760 | tf_op jit(solution)/shard_map/all_gather | solution.py:170
  249.8 25.4 %all-gather.55.cloned.1.call-done = bf16[1,1076,1152]{1,2,0:T(8,128)(2,1)} async-done(((bf16[1,1076,144]{1,2,0:T(8,128)(2,1)}), bf16[1,1076,1152]{1,2,0:T(8,128)(2,1)}) %all-gather.55.cloned.1.call-update) | async-done | bytes 2479120 | tf_op jit(solution)/shard_map/all_gather | solution.py:128
  283.3 35.7 %reduce-scatter.63.cloned.1.call-done = bf16[1,184,1152]{2,1,0:T(8,128)(2,1)} async-done(((bf16[1,736,1152]{2,1,0:T(8,128)(2,1)}), bf16[1,184,1152]{2,1,0:T(8,128)(2,1)}) %reduce-scatter.63.cloned.1.call-update) | async-done | bytes 423952
  334.7 16.9 %all-gather.57.cloned.1.call-done = bf16[1,3,1152,288]{3,2,1,0:T(8,128)(2,1)} async-done(((bf16[1,3,144,288]{3,2,1,0:T(8,128)(2,1)}), bf16[1,3,1152,288]{3,2,1,0:T(8,128)(2,1)}) %all-gather.57.cloned.1.call-update) | async-done | bytes 1990672 | tf_op jit(solution)/shard_map/all_gather | solution.py:118
  351.6 40.2 %all-gather.39.cloned.1.call-done = bf16[1,736,1152]{2,1,0:T(8,128)(2,1)} async-done(((bf16[1,184,1152]{2,1,0:T(8,128)(2,1)}), bf16[1,736,1152]{2,1,0:T(8,128)(2,1)}) %all-gather.39.cloned.1.call-update) | async-done | bytes 1695760 | tf_op jit(solution)/shard_map/all_gather | solution.py:140
  409.7 35.6 %reduce-scatter.65.cloned.1.call-done = bf16[1,184,1152]{2,1,0:T(8,128)(2,1)} async-done(((bf16[1,736,1152]{2,1,0:T(8,128)(2,1)}), bf16[1,184,1152]{2,1,0:T(8,128)(2,1)}) %reduce-scatter.65.cloned.1.call-update) | async-done | bytes 423952
  451.2 26.7 %all-gather.59.cloned.1.call-done = bf16[1,1152,1076]{2,1,0:T(8,128)(2,1)} async-done(((bf16[1,144,1076]{2,1,0:T(8,128)(2,1)}), bf16[1,1152,1076]{2,1,0:T(8,128)(2,1)}) %all-gather.59.cloned.1.call-update) | async-done | bytes 2479120 | tf_op jit(solution)/shard_map/all_gather | solution.py:127
  477.9 40.1 %all-gather.41.cloned.1.call-done = bf16[1,736,1152]{2,1,0:T(8,128)(2,1)} async-done(((bf16[1,184,1152]{2,1,0:T(8,128)(2,1)}), bf16[1,736,1152]{2,1,0:T(8,128)(2,1)}) %all-gather.41.cloned.1.call-update) | async-done | bytes 1695760 | tf_op jit(solution)/shard_map/all_gather | solution.py:170
  524.4 33.7 %all-gather.43.cloned.1.call-done = bf16[1,736,1152]{2,1,0:T(8,128)(2,1)} async-done(((bf16[1,184,1152]{2,1,0:T(8,128)(2,1)}), bf16[1,736,1152]{2,1,0:T(8,128)(2,1)}) %all-gather.43.cloned.1.call-update) | async-done | bytes 1695760 | tf_op jit(solution)/shard_map/all_gather | solution.py:227
  558.0 31.7 %all-gather.61.cloned.1.call-done = bf16[1,1076,1152]{1,2,0:T(8,128)(2,1)} async-done(((bf16[1,1076,144]{1,2,0:T(8,128)(2,1)}), bf16[1,1076,1152]{1,2,0:T(8,128)(2,1)}) %all-gather.61.cloned.1.call-update) | async-done | bytes 2479120 | tf_op jit(solution)/shard_map/all_gather | solution.py:128
  610.7 29.0 %reduce-scatter.69.cloned.1.call-done = bf16[1,184,1152]{2,1,0:T(8,128)(2,1)} async-done(((bf16[1,736,1152]{2,1,0:T(8,128)(2,1)}), bf16[1,184,1152]{2,1,0:T(8,128)(2,1)}) %reduce-scatter.69.cloned.1.call-update) | async-done | bytes 423952
  641.8 36.5 %reduce-scatter.67.cloned.1.call-done = bf16[1,184,1152]{2,1,0:T(8,128)(2,1)} async-done(((bf16[1,736,1152]{2,1,0:T(8,128)(2,1)}), bf16[1,184,1152]{2,1,0:T(8,128)(2,1)}) %reduce-scatter.67.cloned.1.call-update) | async-done | bytes 423952
  683.4 38.2 %all-gather.45.cloned.1.call-done = bf16[1,736,1152]{2,1,0:T(8,128)(2,1)} async-done(((bf16[1,184,1152]{2,1,0:T(8,128)(2,1)}), bf16[1,736,1152]{2,1,0:T(8,128)(2,1)}) %all-gather.45.cloned.1.call-update) | async-done | bytes 1695760 | tf_op jit(solution)/shard_map/all_gather | solution.py:249
  734.1 17.1 %fusion.122 = bf16[4,72,736]{2,1,0:T(8,128)(2,1)S(1)} fusion(f32[4,736,736]{1,2,0:T(8,128)} %fusion.176, f32[4,736,736]{1,2,0:T(8,128)} %copy-done.1, f32[4,736]{1,0:T(4,128)S(1)} %log_add_fusion, pred[736]{0:T(1024)(128)(4,1)S(1)} %compare_reduce_fusion, f32[736,4,72]{0,2,1:T(8,128)} %bitcast.272, f32[4,72]{1,0:T(4,128)S(1)} %reshape.789), kind=kOutput, calls=%fused_computation.138 | convolution fusion | flops 336491104 | bytes 18619744 | tf_op jit(solution)/shard_map/bhqk,bqhd->bkhd/dot_general | solution.py:77
  751.3 18.2 %fusion.222 = (f32[4,72]{1,0:T(4,128)}, bf16[1,736,4,72]{1,3,2,0:T(8,128)(2,1)}) fusion(bf16[736,4,72]{0,2,1:T(8,128)(2,1)S(1)} %bitcast.282, f32[4,736,736]{1,2,0:T(8,128)} %fusion.176, f32[4,736,736]{1,2,0:T(8,128)} %copy-done.1, f32[4,736]{1,0:T(4,128)S(1)} %log_add_fusion, pred[736]{0:T(1024)(128)(4,1)S(1)} %compare_reduce_fusion), kind=kOutput, calls=%fused_computation.295 | convolution fusion | flops 336278848 | bytes 18195808 | tf_op jit(solution)/shard_map/bhqk,bkhd->bqhd/dot_general | solution.py:74
  775.4 36.3 %reduce-scatter.71.cloned.1.call-done = bf16[1,184,1152]{2,1,0:T(8,128)(2,1)} async-done(((bf16[1,736,1152]{2,1,0:T(8,128)(2,1)}), bf16[1,184,1152]{2,1,0:T(8,128)(2,1)}) %reduce-scatter.71.cloned.1.call-update) | async-done | bytes 423952
  817.0 37.8 %all-gather.47.cloned.1.call-done = bf16[1,736,1152]{2,1,0:T(8,128)(2,1)} async-done(((bf16[1,184,1152]{2,1,0:T(8,128)(2,1)}), bf16[1,736,1152]{2,1,0:T(8,128)(2,1)}) %all-gather.47.cloned.1.call-update) | async-done | bytes 1695760 | tf_op jit(solution)/shard_map/all_gather | solution.py:227
  868.3 36.3 %reduce-scatter.73.cloned.1.call-done = bf16[1,184,1152]{2,1,0:T(8,128)(2,1)} async-done(((bf16[1,736,1152]{2,1,0:T(8,128)(2,1)}), bf16[1,184,1152]{2,1,0:T(8,128)(2,1)}) %reduce-scatter.73.cloned.1.call-update) | async-done | bytes 423952
  982.7 17.3 %fusion.220 = (f32[4,72]{1,0:T(4,128)}, bf16[1,736,4,72]{1,3,2,0:T(8,128)(2,1)S(1)}) fusion(bf16[736,4,72]{0,2,1:T(8,128)(2,1)S(1)} %bitcast.280, f32[4,736,736]{1,2,0:T(8,128)} %fusion.174, f32[4,736,736]{1,2,0:T(8,128)} %copy-done, f32[4,736]{1,0:T(4,128)S(1)} %copy-done.36, pred[736]{0:T(1024)(128)(4,1)S(1)} %compare_reduce_fusion), kind=kOutput, calls=%fused_computation.293 | convolution fusion | flops 336278848 | bytes 18195808 | tf_op jit(solution)/shard_map/bhqk,bkhd->bqhd/dot_general | solution.py:74
  1030.5 39.9 %psum.15 = f32[2,4304]{1,0:T(2,128)S(1)} all-reduce(f32[2,4304]{1,0:T(2,128)S(1)} %pad_maximum_fusion.7), channel_id=1, replica_groups=mesh['dp'=8,'tensor'=4] {'dp','tensor'}, use_global_device_ids=true, to_apply=%region_55.56 | all-reduce | flops 8608 | bytes 68864 | tf_op jit(solution)/shard_map/psum | solution.py:339
  1088.1 44.3 %reduce-scatter.51.cloned.1.call-done = bf16[144,1076]{1,0:T(8,128)(2,1)} async-done(((bf16[1152,1076]{1,0:T(8,128)(2,1)}), bf16[144,1076]{1,0:T(8,128)(2,1)}) %reduce-scatter.51.cloned.1.call-update) | async-done | bytes 309904 | tf_op jit(solution)/shard_map/reduce_scatter | solution.py:310
  1132.4 46.4 %reduce-scatter.49.cloned.1.call-done = bf16[144,1076]{1,0:T(8,128)(2,1)} async-done(((bf16[1152,1076]{1,0:T(8,128)(2,1)}), bf16[144,1076]{1,0:T(8,128)(2,1)}) %reduce-scatter.49.cloned.1.call-update) | async-done | bytes 309904 | tf_op jit(solution)/shard_map/reduce_scatter | solution.py:310
  1183.4 33.1 %reduce-scatter.47.cloned.1.call-done = bf16[288,144]{0,1:T(8,128)(2,1)} async-done(((bf16[288,1152]{0,1:T(8,128)(2,1)}), bf16[288,144]{0,1:T(8,128)(2,1)}) %reduce-scatter.47.cloned.1.call-update) | async-done | bytes 82960 | tf_op jit(solution)/shard_map/reduce_scatter | solution.py:307
  1216.5 38.5 %reduce-scatter.45.cloned.1.call-done = bf16[288,144]{0,1:T(8,128)(2,1)} async-done(((bf16[288,1152]{0,1:T(8,128)(2,1)}), bf16[288,144]{0,1:T(8,128)(2,1)}) %reduce-scatter.45.cloned.1.call-update) | async-done | bytes 82960 | tf_op jit(solution)/shard_map/reduce_scatter | solution.py:307
  1256.8 41.8 %reduce-scatter.57.cloned.1.call-done = bf16[144,864]{1,0:T(8,128)(2,1)} async-done(((bf16[1152,864]{1,0:T(8,128)(2,1)}), bf16[144,864]{1,0:T(8,128)(2,1)}) %reduce-scatter.57.cloned.1.call-update) | async-done | bytes 248848
  1304.4 32.7 %reduce-scatter.75.cloned.1.call-done = bf16[1,184,1152]{2,1,0:T(8,128)(2,1)} async-done(((bf16[1,736,1152]{2,1,0:T(8,128)(2,1)}), bf16[1,184,1152]{2,1,0:T(8,128)(2,1)}) %reduce-scatter.75.cloned.1.call-update) | async-done | bytes 423952
  1342.4 123.6 %all-reduce.23.cloned.1.call-done = f32[2,8,1152]{2,0,1:T(2,128)} async-done(((f32[2,8,1152]{2,0,1:T(2,128)}), f32[2,8,1152]{2,0,1:T(2,128)}) %all-reduce.23.cloned.1.call-update) | async-done | bytes 73744 | tf_op jit(solution)/shard_map/psum | solution.py:339
  (405 shorter events, 318.5 us)
Async XLA Ops:
  7.2 77.0 %all-gather.35.cloned.1.call-start = ((), (), s32[]{:S(2)}) async-start(), calls=%async_computation.16 | async-start | bytes 2119680 | tf_op jit(solution)/shard_map/all_gather | solution.py:140
  46.7 69.9 %all-gather.51.cloned.1.call-start = ((), (), s32[]{:S(2)}) async-start(), calls=%async_computation.31 | async-start | bytes 2985984 | tf_op jit(solution)/shard_map/all_gather | solution.py:118
  47.7 123.2 %reduce-scatter.61.cloned.1.call-start = ((), (), s32[]{:S(2)}) async-start(), calls=%async_computation.39 | async-start | bytes 2119680
  134.5 69.0 %all-gather.53.cloned.1.call-start = ((), (), s32[]{:S(2)}) async-start(), calls=%async_computation.32 | async-start | bytes 2985984 | tf_op jit(solution)/shard_map/all_gather | solution.py:127
  135.4 108.1 %all-gather.37.cloned.1.call-start = ((), (), s32[]{:S(2)}) async-start(), calls=%async_computation.17 | async-start | bytes 2119680 | tf_op jit(solution)/shard_map/all_gather | solution.py:170
  173.4 101.8 %all-gather.55.cloned.1.call-start = ((), (), s32[]{:S(2)}) async-start(), calls=%async_computation.33 | async-start | bytes 2985984 | tf_op jit(solution)/shard_map/all_gather | solution.py:128
  174.5 144.5 %reduce-scatter.63.cloned.1.call-start = ((), (), s32[]{:S(2)}) async-start(), calls=%async_computation.40 | async-start | bytes 2119680
  282.5 69.2 %all-gather.57.cloned.1.call-start = ((), (), s32[]{:S(2)}) async-start(), calls=%async_computation.34 | async-start | bytes 2985984 | tf_op jit(solution)/shard_map/all_gather | solution.py:118
  283.2 108.7 %all-gather.39.cloned.1.call-start = ((), (), s32[]{:S(2)}) async-start(), calls=%async_computation.18 | async-start | bytes 2119680 | tf_op jit(solution)/shard_map/all_gather | solution.py:140
  321.5 123.8 %reduce-scatter.65.cloned.1.call-start = ((), (), s32[]{:S(2)}) async-start(), calls=%async_computation.41 | async-start | bytes 2119680
  408.9 69.0 %all-gather.59.cloned.1.call-start = ((), (), s32[]{:S(2)}) async-start(), calls=%async_computation.35 | async-start | bytes 2985984 | tf_op jit(solution)/shard_map/all_gather | solution.py:127
  409.6 108.3 %all-gather.41.cloned.1.call-start = ((), (), s32[]{:S(2)}) async-start(), calls=%async_computation.19 | async-start | bytes 2119680 | tf_op jit(solution)/shard_map/all_gather | solution.py:170
  447.7 110.3 %all-gather.43.cloned.1.call-start = ((), (), s32[]{:S(2)}) async-start(), calls=%async_computation.20 | async-start | bytes 2119680 | tf_op jit(solution)/shard_map/all_gather | solution.py:227
  450.1 139.6 %all-gather.61.cloned.1.call-start = ((), (), s32[]{:S(2)}) async-start(), calls=%async_computation.36 | async-start | bytes 2985984 | tf_op jit(solution)/shard_map/all_gather | solution.py:128
  450.7 189.0 %reduce-scatter.69.cloned.1.call-start = ((), (), s32[]{:S(2)}) async-start(), calls=%async_computation.43 | async-start | bytes 2119680
  603.2 75.2 %reduce-scatter.67.cloned.1.call-start = ((), (), s32[]{:S(2)}) async-start(), calls=%async_computation.42 | async-start | bytes 2119680
  610.6 111.0 %all-gather.45.cloned.1.call-start = ((), (), s32[]{:S(2)}) async-start(), calls=%async_computation.21 | async-start | bytes 2119680 | tf_op jit(solution)/shard_map/all_gather | solution.py:249
  683.4 128.3 %reduce-scatter.71.cloned.1.call-start = ((), (), s32[]{:S(2)}) async-start(), calls=%async_computation.44 | async-start | bytes 2119680
  775.3 79.5 %all-gather.47.cloned.1.call-start = ((), (), s32[]{:S(2)}) async-start(), calls=%async_computation.22 | async-start | bytes 2119680 | tf_op jit(solution)/shard_map/all_gather | solution.py:227
  816.6 88.0 %reduce-scatter.73.cloned.1.call-start = ((), (), s32[]{:S(2)}) async-start(), calls=%async_computation.45 | async-start | bytes 2119680
  868.3 86.6 %all-gather.49.cloned.1.call-start = ((), (), s32[]{:S(2)}) async-start(), calls=%async_computation.23 | async-start | bytes 2119680 | tf_op jit(solution)/shard_map/all_gather | solution.py:249
  910.4 116.7 %reduce-scatter.59.cloned.1.call-start = ((), (), s32[]{:S(2)}) async-start(), calls=%async_computation.38 | async-start | bytes 2322432
  925.6 145.5 %reduce-scatter.55.cloned.1.call-start = ((), (), s32[]{:S(2)}) async-start(), calls=%async_computation.30 | async-start | bytes 2985984 | tf_op jit(solution)/shard_map/reduce_scatter | solution.py:313
  932.6 153.3 %reduce-scatter.53.cloned.1.call-start = ((), (), s32[]{:S(2)}) async-start(), calls=%async_computation.29 | async-start | bytes 2985984 | tf_op jit(solution)/shard_map/reduce_scatter | solution.py:313
  938.9 193.5 %reduce-scatter.51.cloned.1.call-start = ((), (), s32[]{:S(2)}) async-start(), calls=%async_computation.28 | async-start | bytes 2985984 | tf_op jit(solution)/shard_map/reduce_scatter | solution.py:310
  945.2 233.6 %reduce-scatter.49.cloned.1.call-start = ((), (), s32[]{:S(2)}) async-start(), calls=%async_computation.27 | async-start | bytes 2985984 | tf_op jit(solution)/shard_map/reduce_scatter | solution.py:310
  950.8 265.7 %reduce-scatter.47.cloned.1.call-start = ((), (), s32[]{:S(2)}) async-start(), calls=%async_computation.26 | async-start | bytes 995328 | tf_op jit(solution)/shard_map/reduce_scatter | solution.py:307
  954.6 300.4 %reduce-scatter.45.cloned.1.call-start = ((), (), s32[]{:S(2)}) async-start(), calls=%async_computation.25 | async-start | bytes 995328 | tf_op jit(solution)/shard_map/reduce_scatter | solution.py:307
  982.6 315.9 %reduce-scatter.57.cloned.1.call-start = ((), (), s32[]{:S(2)}) async-start(), calls=%async_computation.37 | async-start | bytes 2322432
  1019.2 317.9 %reduce-scatter.75.cloned.1.call-start = ((), (), s32[]{:S(2)}) async-start(), calls=%async_computation.46 | async-start | bytes 2119680
  1025.6 155.5 %copy-start.62 = (f32[4,72]{1,0:T(4,128)S(1)}, f32[4,72]{1,0:T(4,128)}, u32[]{:S(2)}) copy-start(f32[4,72]{1,0:T(4,128)} %get-tuple-element.109) | copy-start | bytes 3460
  1025.6 440.4 %all-reduce.23.cloned.1.call-start = ((), (), s32[]{:S(2)}) async-start(), calls=%async_computation.24 | async-start | bytes 147456 | tf_op jit(solution)/shard_map/psum | solution.py:339
  (73 other events, 1542.5 us)
Sparse Core Ops, SparseCore 0:
  46.9 37.3 all-gather.34
  86.7 29.9 all-gather.50
  134.6 36.3 reduce-scatter.60
  173.3 30.1 all-gather.52
  205.5 38.0 all-gather.36
  245.3 29.9 all-gather.54
  282.6 36.3 reduce-scatter.62
  321.5 30.1 all-gather.56
  353.8 38.0 all-gather.38
  409.0 36.2 reduce-scatter.64
  447.7 30.1 all-gather.58
  479.9 38.0 all-gather.40
  520.1 37.8 all-gather.42
  559.8 29.9 all-gather.60
  603.3 36.3 reduce-scatter.68
  641.9 36.4 reduce-scatter.66
  683.5 38.0 all-gather.44
  775.4 36.2 reduce-scatter.70
  816.7 38.0 all-gather.46
  868.4 36.2 reduce-scatter.72
  910.5 38.0 all-gather.48
  952.0 39.9 reduce-scatter.58
  995.5 43.2 reduce-scatter.54
  1042.1 43.7 reduce-scatter.52
  1089.4 42.9 reduce-scatter.50
  1135.7 42.9 reduce-scatter.48
  1181.8 34.6 reduce-scatter.46
  1220.3 34.6 reduce-scatter.44
  1258.4 40.0 reduce-scatter.56
  1300.7 36.3 reduce-scatter.74
  1342.7 123.3 all-reduce.22
where the time goes:
time: 1480 us
  waiting for transfers between devices  1040 us (70%)
  matrix products  217 us (15%)
  blocking collectives  87.3 us (6%)
  local copies, waits for them, and re-layouts  59.3 us (4%)
  other arithmetic  51.7 us (3%)
  between operations  17 us (1%)
    unnamed x41, waiting for transfers between devices  322 us
    psum x1, waiting for transfers between devices, body(): lax.psum((jnp.stack(vector_list), jnp.stack(expbias_list)), ('dp', 'tenso...  124 us
    reduce_scatter x2, waiting for transfers between devices, body(): lax.psum_scatter(local_grads[2].astype(jnp.bfloat16), 'dp', scatter_dimen...  90.6 us
    all_gather x2, waiting for transfers between devices, body(): lax.all_gather(ff_value.astype(jnp.bfloat16), 'tensor', axis=1, tiled=True)  80.1 us
    reduce_scatter x2, waiting for transfers between devices, body(): lax.psum_scatter(local_grads[1].astype(jnp.bfloat16), 'dp', scatter_dimen...  71.6 us
    all_gather x2, waiting for transfers between devices, body(): upstream_rows = lax.all_gather(upstream_half, 'tensor', axis=1, tiled=True)  71.4 us
    all_gather x2, waiting for transfers between devices, body(): lax.all_gather(mix_value.astype(jnp.bfloat16), 'tensor', axis=1, tiled=True)  66.6 us
    all_gather x2, waiting for transfers between devices, fetch_dense(): lax.all_gather(contract_weight[layer_index], 'dp', axis=1, tiled=True)  57.1 us
  transfers between devices with their start and end apart: 31, of which 28 were waited for; matrix products, arithmetic and copies ran while one was open for 11% of the time, Pallas kernels for 0%

commit v1 on v0

--- a/solution.py
+++ b/solution.py
@@ -1,7 +1,14 @@
+import functools
+
 import jax
 import jax.numpy as jnp
 from jax import lax
+from jax.experimental import pallas as pl
+from jax.experimental.pallas import tpu as pltpu
 from jax.sharding import PartitionSpec as P
+
+
+MESH = pl.DeviceIdType.MESH
 
 HEAD_DIM = 72
 
@@ -78,6 +85,252 @@
         "bhqk,bqhd->bkhd", score_grad, queries, preferred_element_type=jnp.float32
     )
     return (query_grad, key_grad, value_grad)
+
+
+def row_chunks(rows):
+    half = (rows // 2 + 15) // 16 * 16
+    if rows < 32 or half >= rows:
+        return ((0, rows),)
+    return ((0, half), (half, rows - half))
+
+
+def line_barrier(me, size):
+    barrier = pltpu.get_barrier_semaphore()
+
+    @pl.when(me > 0)
+    def _():
+        pl.semaphore_signal(barrier, inc=1, device_id={"tensor": me - 1}, device_id_type=MESH)
+
+    @pl.when(me < size - 1)
+    def _():
+        pl.semaphore_signal(barrier, inc=1, device_id={"tensor": me + 1}, device_id_type=MESH)
+
+    inner = jnp.logical_and(me > 0, me < size - 1)
+
+    @pl.when(inner)
+    def _():
+        pl.semaphore_wait(barrier, 2)
+
+    @pl.when(jnp.logical_not(inner))
+    def _():
+        pl.semaphore_wait(barrier, 1)
+
+
+def gather_kernel(size, chunks, x_ref, o_ref, send_r, send_l, recv_r, recv_l):
+    me = lax.axis_index("tensor")
+    line_barrier(me, size)
+
+    def hop(step, owner, c, rightward):
+        start, rows = chunks[c]
+        span = pl.ds(start, rows)
+        src = x_ref.at[span] if step == 0 else o_ref.at[owner, span]
+        send, recv = (send_r, recv_r) if rightward else (send_l, recv_l)
+        return pltpu.make_async_remote_copy(
+            src_ref=src,
+            dst_ref=o_ref.at[owner, span],
+            send_sem=send.at[step, c],
+            recv_sem=recv.at[owner, c],
+            device_id={"tensor": me + 1 if rightward else me - 1},
+            device_id_type=MESH,
+        )
+
+    for step in range(size):
+        for c in range(len(chunks)):
+            for rightward in (True, False):
+                owner = me - step if rightward else me + step
+                valid = owner >= 0 if rightward else owner <= size - 1
+                has_next = me < size - 1 if rightward else me > 0
+
+                @pl.when(valid)
+                def _():
+                    if step > 0:
+                        hop(step, owner, c, rightward).wait_recv()
+                    if step < size - 1:
+
+                        @pl.when(has_next)
+                        def _():
+                            hop(step, owner, c, rightward).start()
+
+        if step == 0:
+            o_ref[me] = x_ref[...]
+    for step in range(size - 1):
+        for c in range(len(chunks)):
+            for rightward in (True, False):
+                owner = me - step if rightward else me + step
+                valid = owner >= 0 if rightward else owner <= size - 1
+                has_next = me < size - 1 if rightward else me > 0
+
+                @pl.when(jnp.logical_and(valid, has_next))
+                def _():
+                    hop(step, owner, c, rightward).wait_send()
+
+
+def scatter_kernel(size, chunks, p_ref, after_ref, o_ref, acc_r, acc_l, send_r, send_l, recv_r, recv_l):
+    me = lax.axis_index("tensor")
+    line_barrier(me, size)
+
+    def hop(target, c, rightward, first):
+        start, rows = chunks[c]
+        span = pl.ds(start, rows)
+        acc = acc_r if rightward else acc_l
+        send, recv = (send_r, recv_r) if rightward else (send_l, recv_l)
+        return pltpu.make_async_remote_copy(
+            src_ref=p_ref.at[target, span] if first else acc.at[target, span],
+            dst_ref=acc.at[target, span],
+            send_sem=send.at[target, c],
+            recv_sem=recv.at[target, c],
+            device_id={"tensor": me + 1 if rightward else me - 1},
+            device_id_type=MESH,
+        )
+
+    def pass_on(target, c, rightward):
+        start, rows = chunks[c]
+        span = pl.ds(start, rows)
+        acc = acc_r if rightward else acc_l
+        is_first = me == 0 if rightward else me == size - 1
+
+        @pl.when(is_first)
+        def _():
+            hop(target, c, rightward, True).start()
+
+        @pl.when(jnp.logical_not(is_first))
+        def _():
+            hop(target, c, rightward, False).wait_recv()
+            total = acc[target, span].astype(jnp.float32) + p_ref[target, span].astype(jnp.float32)
+            acc[target, span] = total.astype(acc.dtype)
+            hop(target, c, rightward, False).start()
+
+    for step in range(size - 1):
+        for c in range(len(chunks)):
+            target_r, target_l = size - 1 - step, step
+
+            @pl.when(me < target_r)
+            def _():
+                pass_on(target_r, c, True)
+
+            @pl.when(me > target_l)
+            def _():
+                pass_on(target_l, c, False)
+
+    for c, (start, rows) in enumerate(chunks):
+        span = pl.ds(start, rows)
+        o_ref[span] = p_ref[me, span].astype(jnp.float32)
+
+        @pl.when(me > 0)
+        def _():
+            hop(me, c, True, False).wait_recv()
+            o_ref[span] += acc_r[me, span].astype(jnp.float32)
+
+        @pl.when(me < size - 1)
+        def _():
+            hop(me, c, False, False).wait_recv()
+            o_ref[span] += acc_l[me, span].astype(jnp.float32)
+
+    for step in range(size - 1):
+        for c in range(len(chunks)):
+            target_r, target_l = size - 1 - step, step
+
+            @pl.when(me < target_r)
+            def _():
+                hop(target_r, c, True, False).wait_send()
+
+            @pl.when(me > target_l)
+            def _():
+                hop(target_l, c, False, False).wait_send()
+
+
+def exchange_kernel(size, scattered, *refs):
+    count = len(scattered)
+    ins, outs, (send, recv) = refs[:count], refs[count : 2 * count], refs[2 * count :]
+    me = lax.axis_index("dp")
+    barrier = pltpu.get_barrier_semaphore()
+    for step in range(1, size):
+        peer = lax.rem(me + step, size)
+        pl.semaphore_signal(barrier, inc=1, device_id={"dp": peer}, device_id_type=MESH)
+    pl.semaphore_wait(barrier, size - 1)
+
+    def hop(step, part):
+        peer = lax.rem(me + step, size)
+        return pltpu.make_async_remote_copy(
+            src_ref=ins[part].at[peer] if scattered[part] else ins[part],
+            dst_ref=outs[part].at[me],
+            send_sem=send.at[step - 1, part],
+            recv_sem=recv.at[step - 1, part],
+            device_id={"dp": peer},
+            device_id_type=MESH,
+        )
+
+    for step in range(1, size):
+        for part in range(count):
+            hop(step, part).start()
+    for part in range(count):
+        outs[part][me] = ins[part][me] if scattered[part] else ins[part][...]
+    for step in range(1, size):
+        for part in range(count):
+            hop(step, part).wait()
+
+
+VMEM_SPEC = pl.BlockSpec(memory_space=pltpu.VMEM)
+
+
+def call_gather(x, size, collective_id):
+    rows, width = x.shape
+    chunks = row_chunks(rows)
+    sems = [
+        pltpu.SemaphoreType.DMA((size, len(chunks))) for _ in range(4)
+    ]
+    return pl.pallas_call(
+        functools.partial(gather_kernel, size, chunks),
+        out_shape=jax.ShapeDtypeStruct((size, rows, width), x.dtype),
+        in_specs=[VMEM_SPEC],
+        out_specs=VMEM_SPEC,
+        scratch_shapes=sems,
+        cost_estimate=pl.CostEstimate(
+            flops=rows * width * 100000, bytes_accessed=size * rows * width * 2, transcendentals=0
+        ),
+        compiler_params=pltpu.CompilerParams(
+            collective_id=collective_id, has_side_effects=True, vmem_limit_bytes=16 * 1024 * 1024
+        ),
+    )(x)
+
+
+def call_scatter(p, after, collective_id):
+    size, rows, width = p.shape
+    chunks = row_chunks(rows)
+    sems = [
+        pltpu.SemaphoreType.DMA((size, len(chunks))) for _ in range(4)
+    ]
+    return pl.pallas_call(
+        functools.partial(scatter_kernel, size, chunks),
+        out_shape=jax.ShapeDtypeStruct((rows, width), jnp.float32),
+        in_specs=[VMEM_SPEC, pl.BlockSpec(memory_space=pl.ANY)],
+        out_specs=VMEM_SPEC,
+        scratch_shapes=[pltpu.VMEM(p.shape, p.dtype), pltpu.VMEM(p.shape, p.dtype)] + sems,
+        cost_estimate=pl.CostEstimate(
+            flops=rows * width * 100000, bytes_accessed=size * rows * width * 2, transcendentals=0
+        ),
+        compiler_params=pltpu.CompilerParams(
+            collective_id=collective_id, has_side_effects=True, vmem_limit_bytes=24 * 1024 * 1024
+        ),
+    )(p, after)
+
+
+def call_exchange(parts, scattered, size, collective_id):
+    outs = [
+        jax.ShapeDtypeStruct(x.shape if flag else (size,) + x.shape, x.dtype)
+        for x, flag in zip(parts, scattered)
+    ]
+    sem = pltpu.SemaphoreType.DMA((size - 1, len(parts)))
+    return pl.pallas_call(
+        functools.partial(exchange_kernel, size, scattered),
+        out_shape=outs,
+        in_specs=[VMEM_SPEC] * len(parts),
+        out_specs=[VMEM_SPEC] * len(parts),
+        scratch_shapes=[sem, sem],
+        compiler_params=pltpu.CompilerParams(
+            collective_id=collective_id, has_side_effects=True, vmem_limit_bytes=16 * 1024 * 1024
+        ),
+    )(*parts)
 
 
 def body(
@@ -105,31 +358,55 @@
     local_width = inproj_weight.shape[-1]
     local_heads = local_width // HEAD_DIM
     local_hidden = expand_weight.shape[-1]
-    hidden_total = local_hidden * lax.axis_size("tensor")
     shard_width = model_width // lax.axis_size("dp")
     factor = float(HEAD_DIM) ** (-0.5)
     usable = key_valid > 0
-    tensor_index = lax.axis_index("tensor")
-    data_index = lax.axis_index("dp")
     head_shape = (images, seq_total, local_heads, HEAD_DIM)
 
+    tensor_size = lax.axis_size("tensor")
+    data_size = lax.axis_size("dp")
+    vectors = jnp.stack(
+        [mixgain, mixbias, outbias, ffgain, ffbias, conbias]
+    )
+    shared = jnp.pad(
+        vectors.reshape(6 * depth_count, shard_width), ((0, -6 * depth_count % 16), (0, 0))
+    )
+    (vectors_full,) = call_exchange([shared], (False,), data_size, 3)
+    vectors_full = (
+        jnp.swapaxes(vectors_full[:, : 6 * depth_count], 0, 1)
+        .reshape(6, depth_count, model_width)
+    )
+
+    big_gather = jax.jit(lambda x: call_gather(x, tensor_size, 0))
+    big_scatter = jax.jit(lambda p, after: call_scatter(p, after, 1))
+
+    def gather_rows(x):
+        local = x.shape[1]
+        full = big_gather(x.reshape(images * local, model_width))
+        full = full.reshape(tensor_size, images, local, model_width)
+        return jnp.swapaxes(full, 0, 1).reshape(images, seq_total, model_width)
+
+    def scatter_weight(grad, dimension):
+        return lax.psum_scatter(grad, "dp", scatter_dimension=dimension, tiled=True)
+
+    def scatter_rows(p, *earlier):
+        pieces = [x[:1, :128].astype(p.dtype) for x in earlier]
+        pieces += [jnp.zeros((1, 128), p.dtype)] * (8 - len(pieces))
+        after = jnp.concatenate(pieces)
+        local = seq_total // tensor_size
+        split = jnp.swapaxes(p.reshape(images, tensor_size, local, model_width), 0, 1)
+        part = big_scatter(split.reshape(tensor_size, images * local, model_width), after)
+        return part.reshape(images, local, model_width)
+
     def fetch_attention(layer_index):
-        return (
-            lax.all_gather(inproj_weight[layer_index], "dp", axis=1, tiled=True),
-            lax.all_gather(outproj_weight[layer_index], "dp", axis=1, tiled=True),
-            lax.all_gather(mixgain[layer_index], "dp", axis=0, tiled=True),
-            lax.all_gather(mixbias[layer_index], "dp", axis=0, tiled=True),
-            lax.all_gather(outbias[layer_index], "dp", axis=0, tiled=True),
-        )
+        shard = jnp.concatenate([inproj_weight[layer_index], outproj_weight[layer_index].T[None]])
+        full = lax.all_gather(shard, "dp", axis=1, tiled=True)
+        return (full[:3], full[3]) + tuple(vectors_full[:3, layer_index])
 
     def fetch_dense(layer_index):
-        return (
-            lax.all_gather(expand_weight[layer_index], "dp", axis=0, tiled=True),
-            lax.all_gather(contract_weight[layer_index], "dp", axis=1, tiled=True),
-            lax.all_gather(ffgain[layer_index], "dp", axis=0, tiled=True),
-            lax.all_gather(ffbias[layer_index], "dp", axis=0, tiled=True),
-            lax.all_gather(conbias[layer_index], "dp", axis=0, tiled=True),
-        )
+        shard = jnp.stack([expand_weight[layer_index], contract_weight[layer_index].T])
+        full = lax.all_gather(shard, "dp", axis=1, tiled=True)
+        return (full[0], full[1]) + tuple(vectors_full[3:, layer_index])
 
     residual = block_input
     stored = []
@@ -137,7 +414,7 @@
         attention_pack = fetch_attention(layer_index)
         inproj_full, outproj_full, mix_gain, mix_shift, out_shift = attention_pack
         mix_value, mix_normed, mix_inverse = layer_norm(residual, mix_gain, mix_shift)
-        mix_rows = lax.all_gather(mix_value.astype(jnp.bfloat16), "tensor", axis=1, tiled=True)
+        mix_rows = gather_rows(mix_value.astype(jnp.bfloat16))
         projected = jnp.einsum(
             "bsd,cde->cbse", mix_rows, inproj_full, preferred_element_type=jnp.float32
         )
@@ -155,26 +432,24 @@
         heads_out, log_total = attend(queries, keys_half, values_half, usable, factor)
         heads_flat = heads_out.reshape(images, seq_total, local_width)
         partial_out = jnp.einsum(
-            "bse,ed->bsd", heads_flat, outproj_full, preferred_element_type=jnp.float32
+            "bse,de->bsd", heads_flat, outproj_full, preferred_element_type=jnp.float32
         )
         middle = (
             residual
-            + lax.psum_scatter(
-                partial_out.astype(jnp.bfloat16), "tensor", scatter_dimension=1, tiled=True
-            ).astype(jnp.float32)
+            + scatter_rows(partial_out.astype(jnp.bfloat16))
             + out_shift.astype(jnp.float32)
         )
         dense_pack = fetch_dense(layer_index)
         expand_full, contract_full, ff_gain, ff_shift, con_shift = dense_pack
         ff_value, ff_normed, ff_inverse = layer_norm(middle, ff_gain, ff_shift)
-        ff_rows = lax.all_gather(ff_value.astype(jnp.bfloat16), "tensor", axis=1, tiled=True)
+        ff_rows = gather_rows(ff_value.astype(jnp.bfloat16))
         preact = jnp.einsum(
             "bsd,df->bsf", ff_rows, expand_full, preferred_element_type=jnp.float32
         ) + expbias[layer_index].astype(jnp.float32)
         gelu_value, gelu_slope = gelu_parts(preact)
         hidden_half = gelu_value.astype(jnp.bfloat16)
         partial_dense = jnp.einsum(
-            "bsf,fd->bsd", hidden_half, contract_full, preferred_element_type=jnp.float32
+            "bsf,df->bsd", hidden_half, contract_full, preferred_element_type=jnp.float32
         )
         stored.append(
             (
@@ -197,9 +472,7 @@
         )
         residual = (
             middle
-            + lax.psum_scatter(
-                partial_dense.astype(jnp.bfloat16), "tensor", scatter_dimension=1, tiled=True
-            ).astype(jnp.float32)
+            + scatter_rows(partial_dense.astype(jnp.bfloat16))
             + con_shift.astype(jnp.float32)
         )
     upstream = cotangent
@@ -222,15 +495,15 @@
             attention_pack,
             dense_pack,
         ) = stored[layer_index]
-        expand_full, contract_full, ff_gain, ff_shift, con_shift = fetch_dense(layer_index)
+        expand_full, contract_full, ff_gain, ff_shift, con_shift = dense_pack
         upstream_half = upstream.astype(jnp.bfloat16)
-        upstream_rows = lax.all_gather(upstream_half, "tensor", axis=1, tiled=True)
+        upstream_rows = gather_rows(upstream_half)
         contract_grad = jnp.einsum(
-            "bsf,bsd->fd", hidden_half, upstream_rows, preferred_element_type=jnp.float32
+            "bsd,bsf->df", upstream_rows, hidden_half, preferred_element_type=jnp.float32
         )
         preact_grad = (
             jnp.einsum(
-                "bsd,fd->bsf", upstream_rows, contract_full, preferred_element_type=jnp.float32
+                "bsd,df->bsf", upstream_rows, contract_full, preferred_element_type=jnp.float32
             )
             * gelu_slope
         )
@@ -241,17 +514,27 @@
         ff_partial = jnp.einsum(
             "bsf,df->bsd", preact_half, expand_full, preferred_element_type=jnp.float32
         )
-        ff_back = lax.psum_scatter(
-            ff_partial.astype(jnp.bfloat16), "tensor", scatter_dimension=1, tiled=True
-        ).astype(jnp.float32)
+        ff_partial, contract_half, expand_half = lax.optimization_barrier(
+            (
+                ff_partial.astype(jnp.bfloat16),
+                contract_grad.astype(jnp.bfloat16),
+                expand_grad.astype(jnp.bfloat16),
+            )
+        )
+        dense_half = jnp.concatenate([expand_half, contract_half], axis=1)
+        dense_part = scatter_weight(dense_half, 0)
+        ff_back = scatter_rows(ff_partial, dense_half)
         middle_grad = upstream + norm_backward(ff_back, ff_normed, ff_inverse, ff_gain)
-        inproj_full, outproj_full, mix_gain, mix_shift, out_shift = fetch_attention(layer_index)
-        middle_rows = lax.all_gather(middle_grad.astype(jnp.bfloat16), "tensor", axis=1, tiled=True)
+        inproj_full, outproj_full, mix_gain, mix_shift, out_shift = attention_pack
+        middle_rows = gather_rows(middle_grad.astype(jnp.bfloat16))
         outproj_grad = jnp.einsum(
-            "bse,bsd->ed", heads_flat, middle_rows, preferred_element_type=jnp.float32
+            "bsd,bse->de", middle_rows, heads_flat, preferred_element_type=jnp.float32
+        )
+        middle_rows, outproj_half = lax.optimization_barrier(
+            (middle_rows, outproj_grad.astype(jnp.bfloat16))
         )
         heads_grad = (
-            jnp.einsum("bsd,ed->bse", middle_rows, outproj_full, preferred_element_type=jnp.float32)
+            jnp.einsum("bsd,de->bse", middle_rows, outproj_full, preferred_element_type=jnp.float32)
             .astype(jnp.bfloat16)
             .reshape(head_shape)
         )
@@ -263,29 +546,30 @@
         )
         proj_half = proj_grad.astype(jnp.bfloat16)
         inproj_grad = jnp.einsum(
-            "bsd,cbse->cde", mix_rows, proj_half, preferred_element_type=jnp.float32
+            "bsd,cbse->dce", mix_rows, proj_half, preferred_element_type=jnp.float32
         )
         mix_partial = jnp.einsum(
             "cbse,cde->bsd", proj_half, inproj_full, preferred_element_type=jnp.float32
         )
-        mix_back = lax.psum_scatter(
-            mix_partial.astype(jnp.bfloat16), "tensor", scatter_dimension=1, tiled=True
-        ).astype(jnp.float32)
+        mix_partial, inproj_half = lax.optimization_barrier(
+            (mix_partial.astype(jnp.bfloat16), inproj_grad.astype(jnp.bfloat16))
+        )
+        attention_half = jnp.concatenate(
+            [inproj_half.reshape(model_width, 3 * local_width), outproj_half], axis=1
+        )
+        attention_part = scatter_weight(attention_half, 0)
+        mix_back = scatter_rows(mix_partial, attention_half)
         upstream_next = middle_grad + norm_backward(mix_back, mix_normed, mix_inverse, mix_gain)
-        query_full = lax.dynamic_update_slice(
-            jnp.zeros((model_width,), jnp.float32),
-            jnp.sum(proj_grad[0], axis=(0, 1)),
-            (tensor_index * local_width,),
-        )
-        value_full = lax.dynamic_update_slice(
-            jnp.zeros((model_width,), jnp.float32),
-            jnp.sum(proj_grad[2], axis=(0, 1)),
-            (tensor_index * local_width,),
-        )
-        expand_full_bias = lax.dynamic_update_slice(
-            jnp.zeros((hidden_total,), jnp.float32),
-            jnp.sum(preact_grad, axis=(0, 1)),
-            (tensor_index * local_hidden,),
+        query_sum = jnp.sum(proj_grad[0], axis=(0, 1))
+        value_sum = jnp.sum(proj_grad[2], axis=(0, 1))
+        expand_sum = jnp.sum(preact_grad, axis=(0, 1))
+        side = max(local_width, local_hidden)
+        tensor_rows = jnp.stack(
+            [
+                jnp.pad(query_sum, (0, side - local_width)),
+                jnp.pad(value_sum, (0, side - local_width)),
+                jnp.pad(expand_sum, (0, side - local_hidden)),
+            ]
         )
         vector_rows = jnp.stack(
             [
@@ -295,26 +579,20 @@
                 jnp.sum(ff_back * ff_normed, axis=(0, 1)),
                 jnp.sum(ff_back, axis=(0, 1)),
                 jnp.sum(upstream, axis=(0, 1)),
-                query_full,
-                value_full,
             ]
         )
-        local_grads = (inproj_grad, outproj_grad, expand_grad, contract_grad)
-        weight_parts = (
-            lax.psum_scatter(
-                local_grads[0].astype(jnp.bfloat16), "dp", scatter_dimension=1, tiled=True
-            ).astype(jnp.float32),
-            lax.psum_scatter(
-                local_grads[1].astype(jnp.bfloat16), "dp", scatter_dimension=1, tiled=True
-            ).astype(jnp.float32),
-            lax.psum_scatter(
-                local_grads[2].astype(jnp.bfloat16), "dp", scatter_dimension=0, tiled=True
-            ).astype(jnp.float32),
-            lax.psum_scatter(
-                local_grads[3].astype(jnp.bfloat16), "dp", scatter_dimension=1, tiled=True
-            ).astype(jnp.float32),
-        )
-        layer_results[layer_index] = (weight_parts, vector_rows, expand_full_bias)
+        weight_parts = tuple(
+            part.astype(jnp.float32)
+            for part in (
+                jnp.swapaxes(
+                    attention_part[:, : 3 * local_width].reshape(shard_width, 3, local_width), 0, 1
+                ),
+                attention_part[:, 3 * local_width :].T,
+                dense_part[:, :local_hidden],
+                dense_part[:, local_hidden:].T,
+            )
+        )
+        layer_results[layer_index] = (weight_parts, vector_rows, tensor_rows)
         upstream = upstream_next
     inproj_list = []
     outproj_list = []
@@ -323,35 +601,39 @@
     vector_list = []
     expbias_list = []
     for position in range(depth_count):
-        weight_parts, vector_rows, expand_full_bias = layer_results[position]
+        weight_parts, vector_rows, tensor_rows = layer_results[position]
         inproj_list.append(weight_parts[0])
         outproj_list.append(weight_parts[1])
         expand_list.append(weight_parts[2])
         contract_list.append(weight_parts[3])
         vector_list.append(vector_rows)
-        expbias_list.append(expand_full_bias)
+        expbias_list.append(tensor_rows)
     inproj_out, outproj_out, expand_out, contract_out = (
         jnp.stack(inproj_list),
         jnp.stack(outproj_list),
         jnp.stack(expand_list),
         jnp.stack(contract_list),
     )
-    vector_total, expbias_total = lax.psum(
-        (jnp.stack(vector_list), jnp.stack(expbias_list)), ("dp", "tensor")
-    )
-    data_part = lax.dynamic_slice_in_dim(vector_total, data_index * shard_width, shard_width, 2)
-    tensor_part = lax.dynamic_slice_in_dim(vector_total, tensor_index * local_width, local_width, 2)
-    expbias_part = lax.dynamic_slice_in_dim(
-        expbias_total, tensor_index * local_hidden, local_hidden, 1
-    )
+    kinds = 6
+    data_rows = jnp.swapaxes(
+        jnp.stack(vector_list).reshape(depth_count * kinds, data_size, shard_width), 0, 1
+    )
+    tensor_rows = jnp.stack(expbias_list).reshape(depth_count * 3, -1)
+    data_all, tensor_all = call_exchange([data_rows, tensor_rows], (True, False), data_size, 2)
+    tensor_part = jnp.sum(tensor_all, axis=0).reshape(depth_count, 3, -1)
+    data_line = call_gather(jnp.sum(data_all, axis=0), tensor_size, 4)
+    data_part = jnp.sum(data_line, axis=0).reshape(depth_count, kinds, shard_width)
+    query_part = tensor_part[:, 0, :local_width]
+    value_part = tensor_part[:, 1, :local_width]
+    expbias_part = tensor_part[:, 2, :local_hidden]
     return (
         residual,
         upstream,
         data_part[:, 0],
         data_part[:, 1],
         inproj_out,
-        tensor_part[:, 6],
-        tensor_part[:, 7],
+        query_part,
+        value_part,
         outproj_out,
         data_part[:, 2],
         data_part[:, 3],

time: 1480 us -> 895 us (0.60)
  waiting for transfers between devices: 1040 us -> 86.6 us
  Pallas kernels: 0 us -> 494 us
  blocking collectives: 87.3 us -> 0 us
  matrix products: 217 us -> 162 us
  local copies, waits for them, and re-layouts: 59.3 us -> 84 us
    pallas_call x0 -> x19, Pallas kernels: none -> 494 us  [the longest x8 294 us: call_scatter(): pl.pallas_call(functools.partial(scatter_kernel, size, chunks), out_shape...]
    all_gather x14 -> x4, waiting for transfers between devices: 418 us -> 7.88 us  [the longest x2 7.84 us: fetch_attention(): full = lax.all_gather(shard, 'dp', axis=1, tiled=True)]
    unnamed x41 -> x10, waiting for transfers between devices: 322 us -> 0.15 us
    psum x1 -> x0, waiting for transfers between devices: 124 us -> none  [body(): lax.psum((jnp.stack(vector_list), jnp.stack(expbias_list)), ('dp', 'tenso...]
    reduce_scatter x6 -> x2, waiting for transfers between devices: 177 us -> 78.5 us  [scatter_weight(): return lax.psum_scatter(grad, 'dp', scatter_dimension=dimension, tiled=True)]
    psum x1 -> x0, blocking collectives: 39.9 us -> none  [body(): lax.psum((jnp.stack(vector_list), jnp.stack(expbias_list)), ('dp', 'tenso...]
    dot_general x14, matrix products: 68.5 us -> 35.5 us  [the longest x2 10.2 us: body(): jnp.einsum('bsd,df->bsf', upstream_rows, contract_full, preferred_element...]
    unnamed x1 -> x0, blocking collectives: 24.6 us -> none
  transfers between devices with their start and end apart: 31 -> 8, of which waited for: 28 -> 3; matrix products, arithmetic and copies ran while one was open for 11% -> 18% of each run, Pallas kernels for 0% -> 35%
where the time goes in v1:
time: 895 us; the launch traced here: 889 us
  Pallas kernels  494 us (55%)
  matrix products  162 us (18%)
  waiting for transfers between devices  86.6 us (10%)
  local copies, waits for them, and re-layouts  84 us (9%)
  other arithmetic  44.8 us (5%)
  between operations  16.9 us (2%)
    pallas_call x8, Pallas kernels, call_scatter(): pl.pallas_call(functools.partial(scatter_kernel, size, chunks), out_shape...  294 us
    pallas_call x9, Pallas kernels, call_gather(): pl.pallas_call(functools.partial(gather_kernel, size, chunks), out_shape=...  187 us
    reduce_scatter x2, waiting for transfers between devices, scatter_weight(): return lax.psum_scatter(grad, 'dp', scatter_dimension=dimension, tiled=True)  78.5 us
    unnamed x276, local copies, waits for them, and re-layouts  56.2 us
    dot_general x2, matrix products, attend_backward(): jnp.einsum('bhqk,bkhd->bqhd', score_grad, keys_half, preferred_element_ty...  34.7 us
    dot_general x2, matrix products, attend_backward(): jnp.einsum('bhqk,bqhd->bkhd', score_grad, queries, preferred_element_type...  34.3 us
  transfers between devices with their start and end apart: 8, of which 3 were waited for; matrix products, arithmetic and copies ran while one was open for 18% of the time, Pallas kernels for 35%

profile of v1, /device:TPU:8, one launch (start us, length us, event | category | flops | bytes accessed | tf_op | source)
XLA Modules:
  0.0 888.8 jit_solution(1550383584758249001)
XLA Ops:
  24.1 30.1 %_lambda_.16 = bf16[4,184,1152]{2,1,0:T(8,128)(2,1)S(1)} custom-call(bf16[184,1152]{1,0:T(8,128)(2,1)S(1)} %fusion.123.x_ref), custom_call_target="tpu_custom_call" | custom-call | flops 21196800000 | bytes 1695744 | tf_op jit(solution)/shard_map/jit(<lambda>)/pallas_call | solution.py:282
  54.3 7.5 copy.184
  75.1 7.8 all-gather.9.cloned.1.call-done
  92.6 7.3 copy.187
  111.5 38.5 %_lambda_.17 = f32[184,1152]{1,0:T(8,128)S(1)} custom-call(bf16[4,184,1152]{2,1,0:T(8,128)(2,1)S(1)} %bitcast.409, bf16[8,128]{1,0:T(8,128)(2,1)S(1)} %broadcast_16_after_ref.2.after_ref), custom_call_target="tpu_custom_call" | custom-call | flops 21196800000 | bytes 1695744 | tf_op jit(solution)/shard_map/jit(<lambda>)/pallas_call | solution.py:303
  150.8 22.8 %_lambda_.18 = bf16[4,184,1152]{2,1,0:T(8,128)(2,1)S(1)} custom-call(bf16[184,1152]{1,0:T(8,128)(2,1)S(1)} %fusion.124.x_ref), custom_call_target="tpu_custom_call" | custom-call | flops 21196800000 | bytes 1695744 | tf_op jit(solution)/shard_map/jit(<lambda>)/pallas_call | solution.py:282
  181.9 42.5 %_lambda_.19 = f32[184,1152]{1,0:T(8,128)S(1)} custom-call(bf16[4,184,1152]{2,1,0:T(8,128)(2,1)S(1)} %bitcast.410, bf16[8,128]{1,0:T(8,128)(2,1)S(1)} %broadcast_16_after_ref.2.after_ref), custom_call_target="tpu_custom_call" | custom-call | flops 21196800000 | bytes 1695744 | tf_op jit(solution)/shard_map/jit(<lambda>)/pallas_call | solution.py:303
  226.3 16.8 %_lambda_.20 = bf16[4,184,1152]{2,1,0:T(8,128)(2,1)S(1)} custom-call(bf16[184,1152]{1,0:T(8,128)(2,1)S(1)} %fusion.125.x_ref), custom_call_target="tpu_custom_call" | custom-call | flops 21196800000 | bytes 1695744 | tf_op jit(solution)/shard_map/jit(<lambda>)/pallas_call | solution.py:282
  257.1 38.6 %_lambda_.21 = f32[184,1152]{1,0:T(8,128)S(1)} custom-call(bf16[4,184,1152]{2,1,0:T(8,128)(2,1)S(1)} %bitcast.411, bf16[8,128]{1,0:T(8,128)(2,1)S(1)} %broadcast_16_after_ref.2.after_ref), custom_call_target="tpu_custom_call" | custom-call | flops 21196800000 | bytes 1695744 | tf_op jit(solution)/shard_map/jit(<lambda>)/pallas_call | solution.py:303
  296.6 27.3 %_lambda_.24 = bf16[4,184,1152]{2,1,0:T(8,128)(2,1)S(1)} custom-call(bf16[184,1152]{1,0:T(8,128)(2,1)S(1)} %get-tuple-element.200.x_ref), custom_call_target="tpu_custom_call" | custom-call | flops 21196800000 | bytes 1695744 | tf_op jit(solution)/shard_map/jit(<lambda>)/pallas_call | solution.py:282
  323.9 18.3 %_lambda_.22 = bf16[4,184,1152]{2,1,0:T(8,128)(2,1)S(1)} custom-call(bf16[184,1152]{1,0:T(8,128)(2,1)S(1)} %fusion.126.x_ref), custom_call_target="tpu_custom_call" | custom-call | flops 21196800000 | bytes 1695744 | tf_op jit(solution)/shard_map/jit(<lambda>)/pallas_call | solution.py:282
  351.2 5.3 fusion.198
  361.7 5.3 copy.140
  372.3 37.5 %_lambda_.25 = f32[184,1152]{1,0:T(8,128)S(1)} custom-call(bf16[4,184,1152]{2,1,0:T(8,128)(2,1)S(1)} %bitcast.403, bf16[8,128]{1,0:T(8,128)(2,1)S(1)} %concatenate.42.after_ref), custom_call_target="tpu_custom_call" | custom-call | flops 21196800000 | bytes 1695744 | tf_op jit(solution)/shard_map/jit(<lambda>)/pallas_call | solution.py:303
  414.7 36.2 %_lambda_.23 = f32[184,1152]{1,0:T(8,128)S(1)} custom-call(bf16[4,184,1152]{2,1,0:T(8,128)(2,1)S(1)} %bitcast.408, bf16[8,128]{1,0:T(8,128)(2,1)S(1)} %broadcast_16_after_ref.2.after_ref), custom_call_target="tpu_custom_call" | custom-call | flops 21196800000 | bytes 1695744 | tf_op jit(solution)/shard_map/jit(<lambda>)/pallas_call | solution.py:303
  452.9 18.4 %_lambda_.26 = bf16[4,184,1152]{2,1,0:T(8,128)(2,1)S(1)} custom-call(bf16[184,1152]{1,0:T(8,128)(2,1)S(1)} %convert_bitcast_fusion.2.x_ref), custom_call_target="tpu_custom_call" | custom-call | flops 21196800000 | bytes 1695744 | tf_op jit(solution)/shard_map/jit(<lambda>)/pallas_call | solution.py:282
  480.9 17.6 %fusion.83 = bf16[4,72,736]{2,1,0:T(8,128)(2,1)} fusion(f32[4,736,736]{1,2,0:T(8,128)} %fusion.129, f32[4,736,736]{1,2,0:T(8,128)} %copy-done.7, f32[4,736]{1,0:T(4,128)S(1)} %copy-done.68, pred[736]{0:T(1024)(128)(4,1)S(1)} %copy-done.64, f32[736,4,72]{0,2,1:T(8,128)S(1)} %bitcast.424, f32[4,72]{1,0:T(4,128)S(1)} %copy-done.93), kind=kOutput, calls=%fused_computation.101 | convolution fusion | flops 336491104 | bytes 18619744 | tf_op jit(solution)/shard_map/bhqk,bqhd->bkhd/dot_general | solution.py:84
  498.5 17.9 %fusion.187 = (f32[4,72]{1,0:T(4,128)}, bf16[1,736,4,72]{1,3,2,0:T(8,128)(2,1)}) fusion(bf16[736,4,72]{0,2,1:T(8,128)(2,1)S(1)} %bitcast.440, f32[4,736,736]{1,2,0:T(8,128)} %fusion.129, f32[4,736,736]{1,2,0:T(8,128)} %copy-done.7, f32[4,736]{1,0:T(4,128)S(1)} %copy-done.68, pred[736]{0:T(1024)(128)(4,1)S(1)} %copy-done.64), kind=kOutput, calls=%fused_computation.303 | convolution fusion | flops 336278848 | bytes 18195808 | tf_op jit(solution)/shard_map/bhqk,bkhd->bqhd/dot_general | solution.py:81
  524.0 35.3 %_lambda_.27 = f32[184,1152]{1,0:T(8,128)S(1)} custom-call(bf16[4,184,1152]{2,1,0:T(8,128)(2,1)S(1)} %bitcast.399, bf16[8,128]{1,0:T(8,128)(2,1)S(1)} %concatenate.43.after_ref), custom_call_target="tpu_custom_call" | custom-call | flops 21196800000 | bytes 1695744 | tf_op jit(solution)/shard_map/jit(<lambda>)/pallas_call | solution.py:303
  560.3 24.8 %_lambda_.28 = bf16[4,184,1152]{2,1,0:T(8,128)(2,1)S(1)} custom-call(bf16[184,1152]{1,0:T(8,128)(2,1)S(1)} %convert_bitcast_fusion.1.x_ref), custom_call_target="tpu_custom_call" | custom-call | flops 21196800000 | bytes 1695744 | tf_op jit(solution)/shard_map/jit(<lambda>)/pallas_call | solution.py:282
  599.8 33.4 %_lambda_.29 = f32[184,1152]{1,0:T(8,128)S(1)} custom-call(bf16[4,184,1152]{2,1,0:T(8,128)(2,1)S(1)} %bitcast.402, bf16[8,128]{1,0:T(8,128)(2,1)S(1)} %concatenate.44.after_ref), custom_call_target="tpu_custom_call" | custom-call | flops 21196800000 | bytes 1695744 | tf_op jit(solution)/shard_map/jit(<lambda>)/pallas_call | solution.py:303
  636.6 5.2 copy.172
  643.4 18.4 %_lambda_.30 = bf16[4,184,1152]{2,1,0:T(8,128)(2,1)S(1)} custom-call(bf16[184,1152]{1,0:T(8,128)(2,1)S(1)} %convert_bitcast_fusion.x_ref), custom_call_target="tpu_custom_call" | custom-call | flops 21196800000 | bytes 1695744 | tf_op jit(solution)/shard_map/jit(<lambda>)/pallas_call | solution.py:282
  669.1 16.8 %fusion.185 = (f32[4,72]{1,0:T(4,128)S(1)}, bf16[1,736,4,72]{1,3,2,0:T(8,128)(2,1)S(1)}) fusion(bf16[736,4,72]{0,2,1:T(8,128)(2,1)S(1)} %bitcast.438, f32[4,736,736]{1,2,0:T(8,128)} %fusion.127, f32[4,736,736]{1,2,0:T(8,128)} %copy-done.6, f32[4,736]{1,0:T(4,128)S(1)} %copy-done.66, pred[736]{0:T(1024)(128)(4,1)S(1)} %copy-done.64), kind=kOutput, calls=%fused_computation.301 | convolution fusion | flops 336278848 | bytes 18195808 | tf_op jit(solution)/shard_map/bhqk,bkhd->bqhd/dot_general | solution.py:81
  685.9 16.6 %fusion.86 = bf16[4,72,736]{2,1,0:T(8,128)(2,1)S(1)} fusion(f32[4,736,736]{1,2,0:T(8,128)} %fusion.127, f32[4,736,736]{1,2,0:T(8,128)} %copy-done.6, f32[4,736]{1,0:T(4,128)S(1)} %copy-done.66, pred[736]{0:T(1024)(128)(4,1)S(1)} %copy-done.64, f32[736,4,72]{0,2,1:T(8,128)S(1)} %bitcast.422, f32[4,72]{1,0:T(4,128)S(1)} %copy-done.91), kind=kOutput, calls=%fused_computation.102 | convolution fusion | flops 336491104 | bytes 18619744 | tf_op jit(solution)/shard_map/bhqk,bqhd->bkhd/dot_general | solution.py:84
  717.9 6.3 pad_maximum_fusion.1
  724.3 6.7 pad_maximum_fusion
  732.7 32.0 %_lambda_.31 = f32[184,1152]{1,0:T(8,128)S(1)} custom-call(bf16[4,184,1152]{2,1,0:T(8,128)(2,1)S(1)} %bitcast.392, bf16[8,128]{1,0:T(8,128)(2,1)S(1)} %concatenate.45.after_ref), custom_call_target="tpu_custom_call" | custom-call | flops 21196800000 | bytes 1695744 | tf_op jit(solution)/shard_map/jit(<lambda>)/pallas_call | solution.py:303
  765.6 8.1 shard_map.272
  775.6 9.7 %shard_map.273 = f32[4,12,144]{2,1,0:T(8,128)S(1)} custom-call(f32[12,144]{1,0:T(8,128)S(1)} %reduce_sum.419.x_ref), custom_call_target="tpu_custom_call" | custom-call | flops 172800000 | bytes 13824 | tf_op jit(solution)/shard_map/pallas_call | solution.py:282
  798.2 21.5 %reduce-scatter.11.cloned.1.call-done = bf16[144,2152]{1,0:T(8,128)(2,1)} async-done(((bf16[1152,2152]{1,0:T(8,128)(2,1)}), bf16[144,2152]{1,0:T(8,128)(2,1)}) %reduce-scatter.11.cloned.1.call-update) | async-done | bytes 619792 | tf_op jit(solution)/shard_map/reduce_scatter | solution.py:390
  821.0 57.0 %reduce-scatter.9.cloned.1.call-done = bf16[144,2152]{1,0:T(8,128)(2,1)} async-done(((bf16[1152,2152]{1,0:T(8,128)(2,1)}), bf16[144,2152]{1,0:T(8,128)(2,1)}) %reduce-scatter.9.cloned.1.call-update) | async-done | bytes 619792 | tf_op jit(solution)/shard_map/reduce_scatter | solution.py:390
  (476 shorter events, 184.4 us)
Async XLA Ops:
  7.2 47.1 %all-gather.5.cloned.1.call-start = ((), (), s32[]{:S(2)}) async-start(), calls=%async_computation.4 | async-start | bytes 3981312 | tf_op jit(solution)/shard_map/all_gather | solution.py:403
  11.1 71.9 %all-gather.9.cloned.1.call-start = ((), (), s32[]{:S(2)}) async-start(), calls=%async_computation.6 | async-start | bytes 3981312 | tf_op jit(solution)/shard_map/all_gather | solution.py:403
  12.8 160.9 %all-gather.7.cloned.1.call-start = ((), (), s32[]{:S(2)}) async-start(), calls=%async_computation.5 | async-start | bytes 5971968 | tf_op jit(solution)/shard_map/all_gather | solution.py:408
  14.0 328.2 %all-gather.11.cloned.1.call-start = ((), (), s32[]{:S(2)}) async-start(), calls=%async_computation.7 | async-start | bytes 5971968 | tf_op jit(solution)/shard_map/all_gather | solution.py:408
  15.0 775.0 %reduce-scatter.15.cloned.1.call-start = ((), (), s32[]{:S(2)}) async-start(), calls=%async_computation.11 | async-start | bytes 2985984
  15.1 235.2 %copy-start.63 = (pred[736]{0:T(1024)(128)(4,1)}, pred[736]{0:T(1024)(128)(4,1)S(1)}, u32[]{:S(2)}) copy-start(pred[736]{0:T(1024)(128)(4,1)S(1)} %compare_reduce_fusion) | copy-start | bytes 2212
  15.3 39.0 %copy-start.76 = (f32[184]{0:T(256)}, f32[184]{0:T(256)S(1)}, u32[]{:S(2)}) copy-start(f32[184]{0:T(256)S(1)} %broadcast_multiply_fusion.11) | copy-start | bytes 2212
  15.5 38.7 %copy-start.83 = (f32[184]{0:T(256)}, f32[184]{0:T(256)S(1)}, u32[]{:S(2)}) copy-start(f32[184]{0:T(256)S(1)} %add_rsqrt_fusion.3) | copy-start | bytes 2212
  16.3 83.5 %copy-start.90 = (f32[4,72]{1,0:T(4,128)}, f32[4,72]{1,0:T(4,128)S(1)}, u32[]{:S(2)}) copy-start(f32[4,72]{1,0:T(4,128)S(1)} %reshape.930) | copy-start | bytes 3460
  17.1 90.9 %copy-start.59 = (f32[4,72]{1,0:T(4,128)}, f32[4,72]{1,0:T(4,128)S(1)}, u32[]{:S(2)}) copy-start(f32[4,72]{1,0:T(4,128)S(1)} %reshape.929) | copy-start | bytes 3460
  23.9 126.7 %copy-start.52 = (f32[1152]{0:T(1024)}, f32[1152]{0:T(1024)S(1)}, u32[]{:S(2)}) copy-start(f32[1152]{0:T(1024)S(1)} %get-tuple-element.131) | copy-start | bytes 13828
  23.9 201.6 %copy-start.54 = (f32[1152]{0:T(1024)}, f32[1152]{0:T(1024)S(1)}, u32[]{:S(2)}) copy-start(f32[1152]{0:T(1024)S(1)} %get-tuple-element.128) | copy-start | bytes 13828
  67.4 40.6 %copy-start.18 = (f32[1,1,736,288]{2,3,0,1:T(8,128)}, f32[1,1,736,288]{2,3,0,1:T(8,128)S(1)}, u32[]{:S(2)}) copy-start(f32[1,1,736,288]{2,3,0,1:T(8,128)S(1)} %get-tuple-element.155) | copy-start | bytes 2543620
  110.4 39.7 %copy-start.41 = (bf16[4,72,736]{2,1,0:T(8,128)(2,1)}, bf16[4,72,736]{2,1,0:T(8,128)(2,1)S(1)}, u32[]{:S(2)}) copy-start(bf16[4,72,736]{2,1,0:T(8,128)(2,1)S(1)} %convolution_convert_fusion.15) | copy-start | bytes 1271812
  150.3 74.1 %copy-start.12 = (f32[1,184,1152]{2,1,0:T(8,128)}, f32[1,184,1152]{2,1,0:T(8,128)S(1)}, u32[]{:S(2)}) copy-start(f32[1,184,1152]{2,1,0:T(8,128)S(1)} %get-tuple-element.152) | copy-start | bytes 2543620
  181.9 42.5 %copy-start.29 = (f32[1,184,1152]{2,1,0:T(8,128)S(1)}, f32[1,184,1152]{2,1,0:T(8,128)}, u32[]{:S(2)}) copy-start(f32[1,184,1152]{2,1,0:T(8,128)} %param.31) | copy-start | bytes 2543620
  225.2 70.5 %copy-start.14 = (f32[1,184,1152]{2,1,0:T(8,128)}, f32[1,184,1152]{2,1,0:T(8,128)S(1)}, u32[]{:S(2)}) copy-start(f32[1,184,1152]{2,1,0:T(8,128)S(1)} %get-tuple-element.150) | copy-start | bytes 2543620
  257.1 38.7 %copy-start.71 = (f32[1152]{0:T(1024)S(1)}, f32[1152]{0:T(1024)}, u32[]{:S(2)}) copy-start(f32[1152]{0:T(1024)} %get-tuple-element.126) | copy-start | bytes 13828
  367.0 44.3 %slice-start.6 = ((s8[5308416]{0:T(1024)(128)(4,1)}), s8[4194304]{0:T(1024)(128)(4,1)S(1)}, s32[]{:S(2)}) async-start(s8[5308416]{0:T(1024)(128)(4,1)} %bitcast.468), calls=%async_computation.18 | async-start | bytes 8388608
  372.3 38.2 %copy-start.17 = (f32[1,184,1152]{2,1,0:T(8,128)S(1)}, f32[1,184,1152]{2,1,0:T(8,128)}, u32[]{:S(2)}) copy-start(f32[1,184,1152]{2,1,0:T(8,128)} %copy-done.16) | copy-start | bytes 2543620
  372.3 39.1 %slice-start.7 = ((s8[5308416]{0:T(1024)(128)(4,1)}), s8[1114112]{0:T(1024)(128)(4,1)S(1)}, s32[]{:S(2)}) async-start(s8[5308416]{0:T(1024)(128)(4,1)} %bitcast.468), calls=%async_computation.19 | async-start | bytes 2228224
  372.3 39.1 %copy-start.112 = (f32[736,1076]{0,1:T(8,128)S(1)}, f32[736,1076]{0,1:T(8,128)}, u32[]{:S(2)}) copy-start(f32[736,1076]{0,1:T(8,128)} %copy-done.111) | copy-start | bytes 9503236
  414.7 36.3 %copy-start.30 = (f32[1,184,1152]{2,1,0:T(8,128)S(1)}, f32[1,184,1152]{2,1,0:T(8,128)}, u32[]{:S(2)}) copy-start(f32[1,184,1152]{2,1,0:T(8,128)} %param.31) | copy-start | bytes 2543620
  414.7 36.3 %copy-start.69 = (f32[1152]{0:T(1024)S(1)}, f32[1152]{0:T(1024)}, u32[]{:S(2)}) copy-start(f32[1152]{0:T(1024)} %get-tuple-element.123) | copy-start | bytes 13828
  523.9 35.3 %copy-start.55 = (f32[1152]{0:T(1024)S(1)}, f32[1152]{0:T(1024)}, u32[]{:S(2)}) copy-start(f32[1152]{0:T(1024)} %copy-done.54) | copy-start | bytes 13828
  523.9 35.5 %copy-start.15 = (f32[1,184,1152]{2,1,0:T(8,128)S(1)}, f32[1,184,1152]{2,1,0:T(8,128)}, u32[]{:S(2)}) copy-start(f32[1,184,1152]{2,1,0:T(8,128)} %copy-done.14) | copy-start | bytes 2543620
  523.9 35.5 %copy-start.81 = (f32[184]{0:T(256)S(1)}, f32[184]{0:T(256)}, u32[]{:S(2)}) copy-start(f32[184]{0:T(256)} %copy-done.80) | copy-start | bytes 2212
  523.9 35.5 %copy-start.88 = (f32[184]{0:T(256)S(1)}, f32[184]{0:T(256)}, u32[]{:S(2)}) copy-start(f32[184]{0:T(256)} %copy-done.87) | copy-start | bytes 2212
  599.8 34.0 %copy-start.51 = (bf16[1152,288]{0,1:T(8,128)(2,1)S(1)}, bf16[1152,288]{0,1:T(8,128)(2,1)}, u32[]{:S(2)}) copy-start(bf16[1152,288]{0,1:T(8,128)(2,1)} %convolution_convert_fusion.13) | copy-start | bytes 1990660
  641.8 150.9 %reduce-scatter.13.cloned.1.call-start = ((), (), s32[]{:S(2)}) async-start(), calls=%async_computation.10 | async-start | bytes 2985984
  717.6 102.1 %reduce-scatter.11.cloned.1.call-start = ((), (), s32[]{:S(2)}) async-start(), calls=%async_computation.9 | async-start | bytes 5640192 | tf_op jit(solution)/shard_map/reduce_scatter | solution.py:390
  724.3 153.7 %reduce-scatter.9.cloned.1.call-start = ((), (), s32[]{:S(2)}) async-start(), calls=%async_computation.8 | async-start | bytes 5640192 | tf_op jit(solution)/shard_map/reduce_scatter | solution.py:390
  (99 other events, 919.9 us)
Sparse Core Ops, SparseCore 0:
  11.2 35.3 all-gather.4
  49.0 33.8 all-gather.8
  85.4 41.2 all-gather.6
  129.0 41.2 all-gather.10
  641.9 43.8 reduce-scatter.14
  717.7 43.7 reduce-scatter.12
  765.0 54.7 reduce-scatter.10
  823.2 54.7 reduce-scatter.8
